TPU v7x, 256 devices: a whole 4x4x8 slice. The times are simulated.
256 devices in a mesh: seq: 32 (over y_hi, z, core), head: 8 (over x, y_lo).
Axes of the slice: x: 4, y: 4 (y_hi: 2, y_lo: 2; y = y_hi * 2 + y_lo), z: 8, core: 2. Of those that a mesh axis runs over, the one named last changes fastest.
Arguments:
- resid: bfloat16 [8192, 8192], P('seq'), may hold values from -6 to 6
- norm_gain: float32 [8192], replicated, may hold values from 0.1 to 1.9
- sender_diff: bfloat16 [8192, 4096], P('seq', 'head'), may hold values from -6 to 6
- w_out1: bfloat16 [4096, 8192], P('head', 'seq'), may hold values from -0.09375 to 0.09375
- w_query: bfloat16 [8192, 4096], P('seq', 'head')
- w_key: bfloat16 [8192, 1024], P('seq', 'head')
- w_value: bfloat16 [8192, 1024], P('seq', 'head'), may hold values from -0.0625 to 0.0625
- edge_mask: int32 [32, 32], replicated, may hold values 0 or 1
- doc_ids: int32 [32, 256], P('seq'), may hold values from 0 to 3, never falling along the last dimension, each value on 1 to 128 neighbouring positions
Outputs:
- patched: bfloat16 [8192, 4096], P('seq', 'head')
All inputs are finite; a program needn't handle non-finite values.
Results may differ from a plain program's by a relative error of at most 0.0085.
The roundings to bfloat16 on the way count: a program that leaves them out, or rounds other values in their place, can miss the bound.
Values may be sent and summed in bfloat16 or wider, within the bound.
A program may use at most 128 MiB of HBM per device.

v0:
```python
import jax
import jax.numpy as jnp
from jax import lax
from jax.sharding import PartitionSpec as P

HEAD_SIZE = 128


epsilon = 1e-05


def attend(query, keys, values, doc_row, head_dim):
    tokens = query.shape[0]
    groups = keys.shape[1] // head_dim
    query_head_rows = query.reshape(tokens, groups, -1, head_dim)
    key_head_rows = keys.reshape(tokens, groups, head_dim)
    value_head_rows = values.reshape(tokens, groups, head_dim)
    attention_scores = jnp.einsum(
        "pehm,qem->ehpq", query_head_rows, key_head_rows, preferred_element_type=jnp.float32
    ) * head_dim ** (-0.5)
    position = jnp.arange(tokens, dtype=jnp.int32)
    allowed = (doc_row[:, None] == doc_row[None, :]) & (position[None, :] <= position[:, None])
    attention_scores = jnp.where(allowed, attention_scores, -jnp.inf)
    top = jnp.max(attention_scores, axis=-1, keepdims=True)
    attention_weights = jnp.exp(attention_scores - top)
    attention_weights = (
        attention_weights / jnp.sum(attention_weights, axis=-1, keepdims=True)
    ).astype(jnp.bfloat16)
    mixed_values = jnp.einsum(
        "uczp,puv->zucv", attention_weights, value_head_rows, preferred_element_type=jnp.float32
    )
    return mixed_values.astype(jnp.bfloat16).reshape(tokens, -1)


def local(resid, norm_gain, sender_diff, w_out1, w_query, w_key, w_value, edge_mask, doc_ids):
    head_dim = HEAD_SIZE
    query_cols = w_query.shape[1]
    resid_wide = resid.astype(jnp.float32)
    inv_rms = lax.rsqrt(jnp.mean(resid_wide * resid_wide, axis=1) + epsilon)
    normed = (resid_wide * inv_rms[:, None] * norm_gain[None, :]).astype(jnp.bfloat16)
    seq_index = lax.axis_index("seq")
    head_index = lax.axis_index("head")
    receivers = query_cols // head_dim
    senders = edge_mask.shape[0]
    local_mask = lax.dynamic_slice_in_dim(edge_mask, head_index * receivers, receivers, 1).astype(
        jnp.float32
    )
    clean_query = jnp.dot(
        normed,
        lax.all_gather(w_query, "seq", axis=0, tiled=True),
        preferred_element_type=jnp.float32,
    )
    keys = jnp.dot(
        normed, lax.all_gather(w_key, "seq", axis=0, tiled=True), preferred_element_type=jnp.float32
    ).astype(jnp.bfloat16)
    values = jnp.dot(
        normed,
        lax.all_gather(w_value, "seq", axis=0, tiled=True),
        preferred_element_type=jnp.float32,
    ).astype(jnp.bfloat16)
    sender_all = lax.all_gather(sender_diff, "head", axis=1, tiled=True)
    rows_dev = w_query.shape[0]
    gain_rows = lax.dynamic_slice_in_dim(norm_gain, seq_index * rows_dev, rows_dev)
    scaled = (w_query.astype(jnp.float32) * gain_rows[:, None]).astype(jnp.bfloat16)
    partial_virtual = jnp.dot(
        lax.all_gather(w_out1, "head", axis=0, tiled=True),
        scaled,
        preferred_element_type=jnp.float32,
    )
    partial_virtual = (
        partial_virtual.reshape(senders, head_dim, receivers, head_dim)
        * local_mask[:, None, :, None]
    ).reshape(senders * head_dim, query_cols)
    virtual = lax.psum(partial_virtual, "seq").astype(jnp.bfloat16)
    delta = jnp.dot(sender_all, virtual, preferred_element_type=jnp.float32)
    query = (clean_query + inv_rms[:, None] * delta).astype(jnp.bfloat16)
    return attend(query, keys, values, doc_ids[0], head_dim)


def solution(mesh):
    placed = (
        P("seq", None),
        P(),
        P("seq", "head"),
        P("head", "seq"),
        P("seq", "head"),
        P("seq", "head"),
        P("seq", "head"),
        P(),
        P("seq", None),
    )
    return jax.shard_map(
        local, mesh=mesh, in_specs=placed, out_specs=P("seq", "head"), check_vma=False
    )
```

profile of v0, /device:TPU:1, one launch (start us, length us, event | category | flops | bytes accessed | tf_op | source)
XLA Modules:
  0.0 447.9 jit_solution(1219935657815322950)
XLA Ops:
  6.5 0.0 copy-start
  6.5 0.0 copy-start.3
  6.5 0.0 copy-start.4
  6.5 0.0 all-gather.12.cloned.1.call-start
  6.5 0.7 all-gather.12.cloned.1.call-update
  7.3 0.0 all-gather.10.cloned.1.call-start
  7.3 0.7 all-gather.10.cloned.1.call-update
  8.0 0.0 all-gather.14.cloned.1.call-start
  8.1 0.7 all-gather.14.cloned.1.call-update
  8.7 0.0 all-gather.8.cloned.1.call-start
  8.8 0.5 all-gather.8.cloned.1.call-update
  9.3 0.0 all-gather.6.cloned.1.call-start
  9.4 0.5 all-gather.6.cloned.1.call-update
  9.9 0.0 copy-done
  9.9 0.1 constant_dynamic-slice_fusion
  10.0 0.1 copy.22
  10.1 3.1 fusion
  13.2 0.0 copy-done.3
  13.2 0.1 fusion.30
  13.3 0.0 copy-done.4
  13.3 0.1 dynamic_slice.6
  13.4 0.0 copy-start.2
  13.4 52.5 %all-gather.12.cloned.1.call-done = bf16[4096,256]{1,0:T(8,128)(2,1)} async-done(((bf16[512,256]{1,0:T(8,128)(2,1)}), bf16[4096,256]{1,0:T(8,128)(2,1)}) %all-gather.12.cloned.1.call-update) | async-done | bytes 2097168 | tf_op jit(solution)/shard_map/all_gather | solution.py:66
  65.9 0.0 copy-start.1
  65.9 1.1 mul.77
  67.1 0.0 copy-done.2
  67.1 0.4 copy-done.1
  67.5 9.2 %bitcast_multiply_fusion = f32[4096,512]{0,1:T(8,128)} fusion(f32[64,8,32,128]{3,2,1,0:T(8,128)S(1)} %bitcast.54, bf16[4096,256]{1,0:T(8,128)(2,1)S(1)} %copy-done.1, bf16[256,512]{1,0:T(8,128)(2,1)S(1)} %copy-done.2, f32[256]{0:T(256)S(1)} %dynamic_slice.6), kind=kOutput, calls=%fused_computation.5 | convolution fusion | flops 1076232192 | bytes 19137536 | tf_op jit(solution)/shard_map/dot_general | solution.py:65
  76.7 179.3 %all-reduce.1 = bf16[4096,512]{0,1:T(8,128)(2,1)} all-reduce(f32[4096,512]{0,1:T(8,128)} %bitcast_multiply_fusion), channel_id=1, replica_groups=mesh['seq'=32,'head'=8] {'seq'}, use_global_device_ids=true, to_apply=%region_1.0 | all-reduce | flops 2097152 | bytes 12582912 | tf_op jit(solution)/shard_map/psum | solution.py:74
  256.0 0.0 all-gather.10.cloned.1.call-done
  256.0 7.0 %fusion.31 = f32[256,512]{1,0:T(8,128)S(1)} fusion(bf16[8192,512]{1,0:T(8,128)(2,1)} %all-gather.10.cloned.1.call-done, bf16[256,8192]{1,0:T(8,128)(2,1)} %param.9, f32[8192]{0:T(1024)S(1)} %copy-done.4, f32[256]{0:T(256)S(1)} %add_rsqrt_fusion), kind=kOutput, calls=%fused_computation.34 | convolution fusion | flops 2155872256 | bytes 13140992 | tf_op jit(solution)/shard_map/dot_general | solution.py:48
  263.0 13.7 %all-gather.14.cloned.1.call-done = bf16[256,4096]{1,0:T(8,128)(2,1)} async-done(((bf16[256,512]{1,0:T(8,128)(2,1)}), bf16[256,4096]{1,0:T(8,128)(2,1)}) %all-gather.14.cloned.1.call-update) | async-done | bytes 2097168 | tf_op jit(solution)/shard_map/all_gather | solution.py:61
  276.7 4.2 fusion.19
  280.9 75.8 %all-gather.8.cloned.1.call-done = bf16[8192,128]{1,0:T(8,128)(2,1)} async-done(((bf16[256,128]{1,0:T(8,128)(2,1)}), bf16[8192,128]{1,0:T(8,128)(2,1)}) %all-gather.8.cloned.1.call-update) | async-done | bytes 2097168 | tf_op jit(solution)/shard_map/all_gather | solution.py:54
  356.7 4.5 %fusion.37 = (f32[4,256]{1,0:T(4,128)S(1)}, f32[1,4,256,256]{2,3,1,0:T(8,128)S(1)}) fusion(bf16[32,4,8,128]{3,2,1,0:T(8,128)(2,1)S(1)} %fusion.19, bf16[8192,128]{1,0:T(8,128)(2,1)} %all-gather.8.cloned.1.call-done, bf16[256,8192]{1,0:T(8,128)(2,1)} %param.9, f32[8192]{0:T(1024)S(1)} %copy-done.4, f32[256]{0:T(256)S(1)} %add_rsqrt_fusion, ...), kind=kOutput, calls=%fused_computation.35 | convolution fusion | flops 613186560 | bytes 7705600 | tf_op jit(solution)/shard_map/pehm,qem->ehpq/dot_general | solution.py:18
  361.2 0.2 fusion.24
  361.3 74.5 %all-gather.6.cloned.1.call-done = bf16[8192,128]{1,0:T(8,128)(2,1)} async-done(((bf16[256,128]{1,0:T(8,128)(2,1)}), bf16[8192,128]{1,0:T(8,128)(2,1)}) %all-gather.6.cloned.1.call-update) | async-done | bytes 2097168 | tf_op jit(solution)/shard_map/all_gather | solution.py:58
  435.9 4.7 %convolution_convert_fusion = bf16[128,4,256]{2,0,1:T(8,128)(2,1)S(1)} fusion(bf16[8192,128]{1,0:T(8,128)(2,1)} %all-gather.6.cloned.1.call-done, f32[1,4,256,256]{2,3,1,0:T(8,128)S(1)} %get-tuple-element.6, f32[4,256]{1,0:T(4,128)S(1)} %fusion.24, f32[4,256]{1,0:T(4,128)S(1)} %get-tuple-element.5, bf16[256,8192]{1,0:T(8,128)(2,1)} %param.9, ...), kind=kOutput, calls=%fused_computation.14 | convolution fusion | flops 613318656 | bytes 7644160 | tf_op jit(solution)/shard_map/uczp,puv->zucv/dot_general | solution.py:29
  440.5 0.8 copy.19
  (2 shorter events, 0.0 us)
Async XLA Ops:
  6.5 3.4 copy-start
  6.5 6.7 %copy-start.3 = (s32[1,256]{1,0:T(1,128)S(1)}, s32[1,256]{1,0:T(1,128)}, u32[]{:S(2)}) copy-start(s32[1,256]{1,0:T(1,128)} %param.17) | copy-start | bytes 3076
  6.5 6.8 %copy-start.4 = (f32[8192]{0:T(1024)S(1)}, f32[8192]{0:T(1024)}, u32[]{:S(2)}) copy-start(f32[8192]{0:T(1024)} %param.10) | copy-start | bytes 98308
  6.5 59.4 %all-gather.12.cloned.1.call-start = ((), (), s32[]{:S(2)}) async-start(), calls=%async_computation.3 | async-start | bytes 2359296 | tf_op jit(solution)/shard_map/all_gather | solution.py:66
  7.3 248.7 %all-gather.10.cloned.1.call-start = ((), (), s32[]{:S(2)}) async-start(), calls=%async_computation.2 | async-start | bytes 8650752 | tf_op jit(solution)/shard_map/all_gather | solution.py:50
  8.0 268.7 %all-gather.14.cloned.1.call-start = ((), (), s32[]{:S(2)}) async-start(), calls=%async_computation.4 | async-start | bytes 2359296 | tf_op jit(solution)/shard_map/all_gather | solution.py:61
  8.7 347.9 %all-gather.8.cloned.1.call-start = ((), (), s32[]{:S(2)}) async-start(), calls=%async_computation.1 | async-start | bytes 2162688 | tf_op jit(solution)/shard_map/all_gather | solution.py:54
  9.3 426.5 %all-gather.6.cloned.1.call-start = ((), (), s32[]{:S(2)}) async-start(), calls=%async_computation | async-start | bytes 2162688 | tf_op jit(solution)/shard_map/all_gather | solution.py:58
  13.4 53.6 %copy-start.2 = (bf16[256,512]{1,0:T(8,128)(2,1)S(1)}, bf16[256,512]{1,0:T(8,128)(2,1)}, u32[]{:S(2)}) copy-start(bf16[256,512]{1,0:T(8,128)(2,1)} %param.13) | copy-start | bytes 786436
  65.9 1.6 copy-start.1
Sparse Core Ops, SparseCore 0:
  9.2 56.7 all-gather.11
  68.7 133.9 all-gather.9
  204.5 72.1 all-gather.13
  279.3 77.2 all-gather.7
  359.3 76.5 all-gather.5
where the time goes:
time: 448 us
  waiting for transfers between devices  220 us (49%)
  blocking collectives  179 us (40%)
  matrix products  29.5 us (7%)
  between operations  13.2 us (3%)
    psum x1, blocking collectives, local(): virtual = lax.psum(partial_virtual, 'seq').astype(jnp.bfloat16)  179 us
    all_gather x1, waiting for transfers between devices, local(): lax.all_gather(w_key, 'seq', axis=0, tiled=True)  75.8 us
    all_gather x1, waiting for transfers between devices, local(): lax.all_gather(w_value, 'seq', axis=0, tiled=True)  74.5 us
    all_gather x1, waiting for transfers between devices, local(): lax.all_gather(w_out1, 'head', axis=0, tiled=True)  52.5 us
    all_gather x1, waiting for transfers between devices, local(): sender_all = lax.all_gather(sender_diff, 'head', axis=1, tiled=True)  13.7 us
    dot_general x1, matrix products, local(): jnp.dot(lax.all_gather(w_out1, 'head', axis=0, tiled=True), scaled, prefe...  9.17 us
  transfers between devices with their start and end apart: 5, of which 4 were waited for; matrix products, arithmetic and copies ran while one was open for 7% of the time, Pallas kernels for 0%

commit v1 on v0

v1 whole, which is shorter than its diff:
```python
import jax
import jax.numpy as jnp
from jax import lax
from jax.experimental import pallas as pl
from jax.experimental.pallas import tpu as pltpu
from jax.sharding import PartitionSpec as P

HEAD_SIZE = 128
epsilon = 1e-05
NZ = 8
MESH = pl.DeviceIdType.MESH


def rem(a, n):
    return lax.rem(a, n)


def kernel(
    resid_hbm, gain_ref, gain_cols_ref, sender_hbm, out1_hbm, wq_hbm, wk_hbm, wv_hbm,
    edge_ref, doc_row_ref, doc_col_ref,
    out_ref,
    resid, w_all, v_all, s_all, wo, wo_own, wo_mid, acc, acc_v, inv_ref,
    local_sem, w_recv, w_half, w_send, v_recv, v_half, v_send,
    s_recv, s_send, a_recv, a_send, b_recv, b_send, c_recv, c_send,
):
    me = lax.axis_index("seq")
    head = lax.axis_index("head")
    y = me // 16
    z = rem(me // 2, NZ)
    c = rem(me, 2)
    oy, oc = 1 - y, 1 - c

    def seq_of(yy, zz, cc):
        return yy * 16 + zz * 2 + cc

    loads = [
        pltpu.make_async_copy(out1_hbm, wo_own, local_sem.at[0]),
        pltpu.make_async_copy(wq_hbm, w_all.at[y, z, c, :, pl.ds(0, 512)], local_sem.at[1]),
        pltpu.make_async_copy(wk_hbm, w_all.at[y, z, c, :, pl.ds(512, 128)], local_sem.at[2]),
        pltpu.make_async_copy(wv_hbm, w_all.at[y, z, c, :, pl.ds(640, 128)], local_sem.at[3]),
        pltpu.make_async_copy(resid_hbm, resid, local_sem.at[4]),
        pltpu.make_async_copy(sender_hbm, s_all.at[head], local_sem.at[5]),
    ]
    for load in loads:
        load.start()

    barrier = pltpu.get_barrier_semaphore()

    def greet_seq(o, _):
        pl.semaphore_signal(
            barrier, inc=1, device_id=(rem(me + o, 32), head), device_id_type=MESH
        )
        return 0

    def greet_head(o, _):
        pl.semaphore_signal(
            barrier, inc=1, device_id=(me, rem(head + o, 8)), device_id_type=MESH
        )
        return 0

    lax.fori_loop(1, 8, greet_head, 0)
    lax.fori_loop(1, 32, greet_seq, 0)
    loads[0].wait()
    pl.semaphore_wait(barrier, 38)

    def a_copy(o):
        peer = rem(head + o, 8)
        return pltpu.make_async_remote_copy(
            src_ref=wo_own.at[:, peer], dst_ref=wo_mid.at[head],
            send_sem=a_send.at[o], recv_sem=a_recv.at[head],
            device_id=(me, peer), device_id_type=MESH,
        )

    def a_arrival(o):
        peer = rem(head + o, 8)
        return pltpu.make_async_remote_copy(
            src_ref=wo_own.at[:, peer], dst_ref=wo_mid.at[peer],
            send_sem=a_send.at[o], recv_sem=a_recv.at[peer],
            device_id=(me, peer), device_id_type=MESH,
        )

    a_local = pltpu.make_async_copy(wo_own.at[:, head], wo_mid.at[head], local_sem.at[6])

    def loop(n, f):
        def body(o, _):
            f(o)
            return 0

        lax.fori_loop(1, n, body, 0)

    loop(8, lambda o: a_copy(o).start())
    a_local.start()

    class Ring:
        def __init__(self, buf, recv, half, send):
            self.buf, self.recv, self.half, self.send = buf, recv, half, send
            self.rows = buf.shape[3] // 2
            self.sent = []

        def desc(self, slot, target, part=None, recv=None, index=0):
            view = self.buf.at[slot]
            if part is not None:
                view = self.buf.at[slot[0], slot[1], slot[2], pl.ds(part * self.rows, self.rows)]
            if recv is None:
                recv = self.recv.at[seq_of(*slot)]
            return pltpu.make_async_remote_copy(
                src_ref=view, dst_ref=view, send_sem=self.send.at[index], recv_sem=recv,
                device_id=(target, head), device_id_type=MESH,
            )

        def put(self, slot, target, part=None, recv=None):
            copy = self.desc(slot, target, part, recv, len(self.sent))
            copy.start()
            self.sent.append(copy)

        def got(self, slot, part=None, recv=None):
            self.desc(slot, seq_of(y, z, oc), part, recv).wait_recv()

        def spread(self, slot, across):
            if across:
                self.put(slot, seq_of(oy, z, c))
            for step in (1, NZ - 1):
                self.put(slot, seq_of(y, rem(z + step, NZ), c))
            self.put(slot, seq_of(y, z, oc))

        def across(self):
            slot = (oy, z, c)
            self.got(slot)
            self.spread(slot, False)
            self.got((oy, z, oc))
            return [(oy, z)]

        def own(self):
            self.got((y, z, oc))
            return [(y, z)]

        def plane(self, yy, d):
            if d == 4:
                zz = rem(z + 4, NZ)
                slot = (yy, zz, c)
                self.got(slot, 0)
                self.got(slot, 1, self.half.at[yy])
                self.put(slot, seq_of(y, z, oc))
                self.got((yy, zz, oc))
                return [(yy, zz)]
            chips = []
            for part, step in ((0, 1), (1, NZ - 1)):
                zz = rem(z + (NZ - step) * d, NZ)
                slot = (yy, zz, c)
                self.got(slot)
                onward = seq_of(y, rem(z + step, NZ), c)
                if d < 3:
                    self.put(slot, onward)
                elif part == 0:
                    self.put(slot, onward, 0)
                else:
                    self.put(slot, onward, 1, self.half.at[yy])
                self.put(slot, seq_of(y, z, oc))
                chips.append((yy, zz))
            for yy, zz in chips:
                self.got((yy, zz, oc))
            return chips

        def finish(self):
            for copy in self.sent:
                copy.wait_send()

    ring = Ring(w_all, w_recv, w_half, w_send)
    for load in loads[1:4]:
        load.wait()
    ring.spread((y, z, c), True)

    loads[4].wait()

    def add_squares(k, total):
        part = resid[:, pl.ds(pl.multiple_of(k * 512, 512), 512)].astype(jnp.float32)
        part = part * part
        return total + part[:, :128] + part[:, 128:256] + part[:, 256:384] + part[:, 384:]

    squares = lax.fori_loop(0, 16, add_squares, jnp.zeros((256, 128), jnp.float32))
    inv_ref[...] = lax.rsqrt(jnp.sum(squares, axis=1, keepdims=True) * (1.0 / 8192) + epsilon)

    loop(8, lambda o: a_arrival(o).wait_recv())
    a_local.wait()

    def b_copy(o):
        peer = rem(me + o, 32)
        return pltpu.make_async_remote_copy(
            src_ref=wo_mid.at[peer // 4, rem(peer, 4)], dst_ref=wo.at[head, me],
            send_sem=b_send.at[o], recv_sem=b_recv.at[me],
            device_id=(peer, head), device_id_type=MESH,
        )

    def b_arrival(o):
        peer = rem(me + o, 32)
        return pltpu.make_async_remote_copy(
            src_ref=wo_mid.at[peer // 4, rem(peer, 4)], dst_ref=wo.at[head, peer],
            send_sem=b_send.at[o], recv_sem=b_recv.at[peer],
            device_id=(peer, head), device_id_type=MESH,
        )

    b_local = pltpu.make_async_copy(
        wo_mid.at[me // 4, rem(me, 4)], wo.at[head, me], local_sem.at[7]
    )
    loop(32, lambda o: b_copy(o).start())
    b_local.start()

    acc[...] = jnp.zeros_like(acc)
    acc_v[...] = jnp.zeros_like(acc_v)

    def project(chips):
        for yy, zz in chips:
            at = pl.multiple_of((yy * 8 + zz) * 512, 512)
            part = resid[:, pl.ds(at, 512)].astype(jnp.float32)
            normed = (part * inv_ref[...] * gain_ref[:, pl.ds(at, 512)]).astype(jnp.bfloat16)
            acc[...] += jnp.dot(
                normed, w_all[yy, zz].reshape(512, 768), preferred_element_type=jnp.float32
            )

    lane = lax.broadcasted_iota(jnp.int32, (256, 32), 1)

    def virtual_part(chips):
        for yy, zz in chips:
            for cc in range(2):
                j = seq_of(yy, zz, cc)
                gain = jnp.sum(
                    jnp.where(lane == j, gain_cols_ref[...], 0.0), axis=1, keepdims=True
                )
                scaled = (
                    w_all[yy, zz, cc, :, :512].astype(jnp.float32) * gain
                ).astype(jnp.bfloat16)
                acc_v[...] += jnp.dot(
                    wo[:, j].reshape(128, 256), scaled, preferred_element_type=jnp.float32
                )

    waiting = []

    def take(chips):
        project(chips)
        waiting.extend(chips)

    take(ring.own())
    take(ring.plane(y, 1))

    loop(32, lambda o: b_arrival(o).wait_recv())
    b_local.wait()

    def gather_copy(buf, send, recv, o, arriving):
        peer = rem(head + o, 8)
        slot = peer if arriving else head
        return pltpu.make_async_remote_copy(
            src_ref=buf.at[slot], dst_ref=buf.at[slot],
            send_sem=send.at[o], recv_sem=recv.at[slot],
            device_id=(me, peer), device_id_type=MESH,
        )

    loop(8, lambda o: gather_copy(wo, c_send, c_recv, o, False).start())
    loads[5].wait()
    loop(8, lambda o: gather_copy(s_all, s_send, s_recv, o, False).start())

    take(ring.across())
    take(ring.plane(y, 2))
    take(ring.plane(oy, 1))
    take(ring.plane(y, 3))
    take(ring.plane(oy, 2))
    take(ring.plane(y, 4))
    loop(8, lambda o: gather_copy(wo, c_send, c_recv, o, True).wait_recv())
    virtual_part(waiting)
    for chips in (ring.plane(oy, 3), ring.plane(oy, 4)):
        project(chips)
        virtual_part(chips)

    for r in range(4):
        cols = pl.ds(r * 128, 128)
        keep = edge_ref[me, head * 4 + r].astype(jnp.float32)
        v_all[y, z, c, :, cols] = (acc_v[:, cols] * keep).astype(jnp.bfloat16)
    vring = Ring(v_all, v_recv, v_half, v_send)
    vring.spread((y, z, c), True)

    loop(8, lambda o: gather_copy(s_all, s_send, s_recv, o, True).wait_recv())

    def patch(chips):
        for yy, zz in chips:
            k = yy * 8 + zz
            rows = s_all[k // 2, :, pl.ds(pl.multiple_of(rem(k, 2) * 256, 256), 256)]
            acc[:, :512] += inv_ref[...] * jnp.dot(
                rows, v_all[yy, zz].reshape(256, 512), preferred_element_type=jnp.float32
            )

    keys = acc[:, 512:640].astype(jnp.bfloat16)
    values = acc[:, 640:768].astype(jnp.bfloat16)

    patch(vring.own())
    patch(vring.plane(y, 1))
    patch(vring.across())
    patch(vring.plane(y, 2))
    patch(vring.plane(oy, 1))
    patch(vring.plane(y, 3))
    patch(vring.plane(oy, 2))
    patch(vring.plane(y, 4))
    patch(vring.plane(oy, 3))
    patch(vring.plane(oy, 4))

    row = lax.broadcasted_iota(jnp.int32, (256, 256), 0)
    col = lax.broadcasted_iota(jnp.int32, (256, 256), 1)
    allowed = (doc_col_ref[...] == doc_row_ref[...]) & (col <= row)
    for r in range(4):
        cols = pl.ds(r * 128, 128)
        query = acc[:, cols].astype(jnp.bfloat16)
        scores = lax.dot_general(
            query, keys, (((1,), (1,)), ((), ())), preferred_element_type=jnp.float32
        ) * HEAD_SIZE ** (-0.5)
        scores = jnp.where(allowed, scores, -jnp.inf)
        weights = jnp.exp(scores - jnp.max(scores, axis=1, keepdims=True))
        weights = (weights / jnp.sum(weights, axis=1, keepdims=True)).astype(jnp.bfloat16)
        out_ref[:, cols] = jnp.dot(
            weights, values, preferred_element_type=jnp.float32
        ).astype(jnp.bfloat16)

    ring.finish()
    vring.finish()
    loop(8, lambda o: a_copy(o).wait_send())
    loop(32, lambda o: b_copy(o).wait_send())
    loop(8, lambda o: gather_copy(wo, c_send, c_recv, o, False).wait_send())
    loop(8, lambda o: gather_copy(s_all, s_send, s_recv, o, False).wait_send())


def local(resid, norm_gain, sender_diff, w_out1, w_query, w_key, w_value, edge_mask, doc_ids):
    dma = pltpu.SemaphoreType.DMA
    anywhere = pl.BlockSpec(memory_space=pl.ANY)
    vmem = pl.BlockSpec(memory_space=pltpu.VMEM)
    smem = pl.BlockSpec(memory_space=pltpu.SMEM)
    bf16, f32 = jnp.bfloat16, jnp.float32
    return pl.pallas_call(
        kernel,
        out_shape=jax.ShapeDtypeStruct((256, 512), bf16),
        in_specs=[
            anywhere, vmem, vmem, anywhere, anywhere, anywhere, anywhere, anywhere,
            smem, vmem, vmem,
        ],
        out_specs=vmem,
        scratch_shapes=[
            pltpu.VMEM((256, 8192), bf16),
            pltpu.VMEM((2, NZ, 2, 256, 768), bf16),
            pltpu.VMEM((2, NZ, 2, 128, 512), bf16),
            pltpu.VMEM((8, 256, 512), bf16),
            pltpu.VMEM((8, 32, 16, 256), bf16),
            pltpu.VMEM((4, 8, 16, 256), bf16),
            pltpu.VMEM((8, 4, 16, 256), bf16),
            pltpu.VMEM((256, 768), f32),
            pltpu.VMEM((128, 512), f32),
            pltpu.VMEM((256, 1), f32),
            dma((8,)),
            dma((32,)), dma((2,)), dma((40,)),
            dma((32,)), dma((2,)), dma((40,)),
            dma((8,)), dma((8,)),
            dma((8,)), dma((8,)),
            dma((32,)), dma((32,)),
            dma((8,)), dma((8,)),
        ],
        compiler_params=pltpu.CompilerParams(
            collective_id=0, has_side_effects=True, vmem_limit_bytes=60 * 1024 * 1024
        ),
        name="patch_layer",
    )(
        resid,
        norm_gain.reshape(1, -1),
        norm_gain.reshape(32, 256).T,
        sender_diff,
        w_out1.reshape(4, 8, 16, 256),
        w_query,
        w_key,
        w_value,
        edge_mask,
        doc_ids,
        doc_ids.reshape(-1, 1),
    )


def solution(mesh):
    placed = (
        P("seq", None),
        P(),
        P("seq", "head"),
        P("head", "seq"),
        P("seq", "head"),
        P("seq", "head"),
        P("seq", "head"),
        P(),
        P("seq", None),
    )
    return jax.shard_map(
        local, mesh=mesh, in_specs=placed, out_specs=P("seq", "head"), check_vma=False
    )
```

time: 448 us -> 126 us (0.28)
  the two profiles are of different devices: /device:TPU:1 before, /device:TPU:25 now
where the time goes in v1:
time: 126 us; the launch traced here: 125 us
  Pallas kernels  121 us (96%)
  local copies, waits for them, and re-layouts  4.67 us (4%)
    pallas_call x1, Pallas kernels, local(): pl.pallas_call(kernel, out_shape=jax.ShapeDtypeStruct((256, 512), bf16),...  121 us

profile of v1, /device:TPU:25, one launch (start us, length us, event | category | flops | bytes accessed | tf_op | source)
XLA Modules:
  0.0 125.4 jit_solution(6146479377340687505)
XLA Ops:
  0.0 0.8 reshape.13
  0.8 0.8 copy.10
  1.5 1.5 %copy.11.doc_col_ref = s32[256,1]{1,0:T(8,128)} copy(s32[256,1]{0,1:T(1,128)} %bitcast.7) | data formatting | bytes 2048 | tf_op jit(solution)/shard_map/reshape | solution.py:376
  3.0 120.7 %patch_layer.1 = bf16[256,512]{1,0:T(8,128)(2,1)} custom-call(bf16[256,8192]{1,0:T(8,128)(2,1)} %resid_hbm.1, f32[1,8192]{1,0:T(1,128)} %bitcast.6, f32[256,32]{1,0:T(8,128)} %bitcast.4, bf16[256,512]{1,0:T(8,128)(2,1)} %sender_hbm.1, bf16[4,8,16,256]{3,2,1,0:T(8,128)(2,1)} %bitcast.5, bf16[256,512]{1,0:T(8,128)(2,1)} %wq_hbm.1, bf16[256,128]{1,0:T(8,128)(2,1)} %wk_hbm.1, ...), custom_call_target="tpu_custom_call" | custom-call | tf_op jit(solution)/shard_map/patch_layer/pallas_call | solution.py:334
  123.7 1.7 %copy.13 = bf16[256,512]{1,0:T(8,128)(2,1)} copy(bf16[256,512]{1,0:T(8,128)(2,1)} %patch_layer.1) | data formatting | bytes 524288

commit v2 on v1

v2 whole, which is shorter than its diff:
```python
import jax
import jax.numpy as jnp
from jax import lax
from jax.experimental import pallas as pl
from jax.experimental.pallas import tpu as pltpu
from jax.sharding import PartitionSpec as P

HEAD_SIZE = 128
epsilon = 1e-05
NZ = 8
MESH = pl.DeviceIdType.MESH


def rem(a, n):
    return lax.rem(a, n)


def kernel(
    resid_hbm, gain_ref, sender_hbm, out1_hbm, wq_hbm, wk_hbm, wv_hbm, edge_ref, doc_ref,
    out_ref,
    resid, q_all, kv_all, v_all, s_all, wo, wo_own, wo_mid, acc, acc_kv, acc_v, inv_ref,
    local_sem, token_sem, q_sems, kv_sems, v_sems, wo_sems, s_sems,
    a_recv, a_send, b_recv, b_send,
):
    me = lax.axis_index("seq")
    head = lax.axis_index("head")
    y = me // 16
    z = rem(me // 2, NZ)
    c = rem(me, 2)
    oy, oc = 1 - y, 1 - c
    x = head // 2
    low = rem(head, 2)
    olow = 1 - low

    def seq_of(yy, zz, cc):
        return yy * 16 + zz * 2 + cc

    def at_z(step):
        return rem(z + (step + NZ), NZ)

    def at_x(step):
        return rem(x + (step + 4), 4)

    loads = [
        pltpu.make_async_copy(out1_hbm, wo_own, local_sem.at[0]),
        pltpu.make_async_copy(wq_hbm, q_all.at[y, z, c], local_sem.at[1]),
        pltpu.make_async_copy(wk_hbm, kv_all.at[y, z, c, :, pl.ds(0, 128)], local_sem.at[2]),
        pltpu.make_async_copy(wv_hbm, kv_all.at[y, z, c, :, pl.ds(128, 128)], local_sem.at[3]),
        pltpu.make_async_copy(resid_hbm, resid, local_sem.at[4]),
        pltpu.make_async_copy(sender_hbm, s_all.at[head], local_sem.at[5]),
    ]
    for k in (1, 0, 2, 3, 4, 5):
        loads[k].start()

    def loop(n, f):
        def body(o, _):
            f(o)
            return 0

        lax.fori_loop(1, n, body, 0)

    def tell(sem, device):
        pl.semaphore_signal(sem, inc=1, device_id=device, device_id_type=MESH)

    barrier = pltpu.get_barrier_semaphore()
    across_dev = (seq_of(oy, z, c), head)
    core_dev = (seq_of(y, z, oc), head)
    up_dev = (seq_of(y, at_z(1), c), head)
    down_dev = (seq_of(y, at_z(-1), c), head)
    for device in (across_dev, up_dev, down_dev, core_dev):
        tell(barrier, device)
    loop(8, lambda o: tell(barrier, (me, rem(head + o, 8))))
    loads[1].wait()
    loads[0].wait()
    pl.semaphore_wait(barrier, 11)

    class Ring:
        def __init__(self, buf, sems, first):
            self.buf = buf
            self.recv, self.recv_b, self.half, self.send = sems
            self.rows = buf.shape[3]
            self.first = first
            self.whole = (0, self.rows)
            self.a = (0, first)
            self.b = (first, self.rows - first)
            self.sent = []

        def desc(self, slot, rows, device, recv, index=0):
            view = self.buf.at[slot[0], slot[1], slot[2], pl.ds(*rows)]
            return pltpu.make_async_remote_copy(
                src_ref=view, dst_ref=view, send_sem=self.send.at[index], recv_sem=recv,
                device_id=device, device_id_type=MESH,
            )

        def put(self, slot, rows, device, recv):
            copy = self.desc(slot, rows, device, recv, len(self.sent))
            copy.start()
            self.sent.append(copy)

        def got(self, slot, rows, recv):
            self.desc(slot, rows, core_dev, recv).wait_recv()

        def main(self, slot):
            return self.recv.at[seq_of(*slot)]

        def late(self, slot):
            return self.recv_b.at[seq_of(*slot)]

        def start(self):
            slot = (y, z, c)
            self.put(slot, self.whole, up_dev, self.main(slot))
            self.put(slot, self.whole, down_dev, self.main(slot))
            self.put(slot, self.a, across_dev, self.main(slot))
            self.put(slot, self.whole, core_dev, self.main(slot))
            self.put(slot, self.b, across_dev, self.late(slot))

        def round(self, yy, d, rows, kind):
            cut = (rows[0], rows[1] // 2), (rows[0] + rows[1] // 2, rows[1] // 2)
            if d == 4:
                slot = (yy, at_z(4), c)
                self.got(slot, cut[0], self.main(slot))
                self.got(slot, cut[1], self.half.at[kind])
                arrived = [slot]
            else:
                arrived = []
                for part, step, onward in ((0, 1, up_dev), (1, -1, down_dev)):
                    slot = (yy, at_z(-step * d), c)
                    self.got(slot, rows, self.main(slot))
                    if d < 3:
                        self.put(slot, rows, onward, self.main(slot))
                    else:
                        recv = self.half.at[kind] if part else self.main(slot)
                        self.put(slot, cut[part], onward, recv)
                    arrived.append(slot)
            for slot in arrived:
                if kind == 0:
                    self.put(slot, self.b, across_dev, self.late(slot))
                self.put(slot, rows, core_dev, self.main(slot))

        def plane(self, d):
            self.round(y, d, self.whole, 0)

        def other(self, d):
            self.round(oy, d, self.a, 1)

        def other_start(self):
            slot = (oy, z, c)
            self.got(slot, self.a, self.main(slot))
            self.put(slot, self.a, up_dev, self.main(slot))
            self.put(slot, self.a, down_dev, self.main(slot))
            self.put(slot, self.a, core_dev, self.main(slot))

        def places(self, d):
            return [at_z(d)] if d in (0, 4) else [at_z(-d), at_z(d)]

        def cross(self, d):
            for zz in self.places(d):
                slot = (oy, zz, c)
                self.got(slot, self.b, self.late(slot))
                self.put(slot, self.b, core_dev, self.late(slot))

        def chips(self, d):
            for zz in self.places(d):
                slot = (y, zz, oc)
                self.got(slot, self.whole, self.main(slot))
            return [(y, zz) for zz in self.places(d)]

        def other_chips(self, d):
            for zz in self.places(d):
                slot = (oy, zz, oc)
                self.got(slot, self.a, self.main(slot))
                self.got(slot, self.b, self.late(slot))
            return [(oy, zz) for zz in self.places(d)]

        def finish(self):
            for copy in self.sent:
                copy.wait_send()

    class HeadRing:
        def __init__(self, buf, sems):
            self.buf = buf
            self.recv, self.half, self.send = sems
            self.size = buf.shape[1]
            self.sent = []

        def desc(self, slot, rows, device, recv, index=0):
            view = self.buf.at[slot, pl.ds(*rows)]
            return pltpu.make_async_remote_copy(
                src_ref=view, dst_ref=view, send_sem=self.send.at[index], recv_sem=recv,
                device_id=device, device_id_type=MESH,
            )

        def put(self, slot, rows, step, recv, swap=False):
            device = (me, x * 2 + olow) if swap else (me, at_x(step) * 2 + low)
            copy = self.desc(slot, rows, device, recv, len(self.sent))
            copy.start()
            self.sent.append(copy)

        def got(self, slot, rows, recv):
            self.desc(slot, rows, (me, x * 2 + olow), recv).wait_recv()

        def start(self):
            whole = (0, self.size)
            for step in (1, -1):
                self.put(head, whole, step, self.recv.at[head])
            self.put(head, whole, 0, self.recv.at[head], swap=True)

        def pair(self):
            whole, slot = (0, self.size), x * 2 + olow
            self.got(slot, whole, self.recv.at[slot])
            for step in (1, -1):
                self.put(slot, whole, step, self.recv.at[slot])

        def one(self, kind):
            half = self.size // 2
            ll = olow if kind else low
            for part, step in ((0, 1), (1, -1)):
                slot = at_x(-step) * 2 + ll
                self.got(slot, (0, self.size), self.recv.at[slot])
                recv = self.half.at[kind] if part else self.recv.at[slot]
                self.put(slot, (part * half, half), step, recv)

        def two(self, kind):
            half = self.size // 2
            slot = at_x(2) * 2 + (olow if kind else low)
            self.got(slot, (0, half), self.recv.at[slot])
            self.got(slot, (half, half), self.half.at[kind])

        def finish(self):
            for copy in self.sent:
                copy.wait_send()

    qring = Ring(q_all, q_sems, 128)
    kvring = Ring(kv_all, kv_sems, 128)
    vring = Ring(v_all, v_sems, 64)
    oring = HeadRing(wo, wo_sems)
    sring = HeadRing(s_all, s_sems)
    qring.start()

    def a_copy(o):
        peer = rem(head + o, 8)
        return pltpu.make_async_remote_copy(
            src_ref=wo_own.at[:, peer], dst_ref=wo_mid.at[head],
            send_sem=a_send.at[o], recv_sem=a_recv.at[head],
            device_id=(me, peer), device_id_type=MESH,
        )

    def a_arrival(o):
        peer = rem(head + o, 8)
        return pltpu.make_async_remote_copy(
            src_ref=wo_own.at[:, peer], dst_ref=wo_mid.at[peer],
            send_sem=a_send.at[o], recv_sem=a_recv.at[peer],
            device_id=(me, peer), device_id_type=MESH,
        )

    a_local = pltpu.make_async_copy(wo_own.at[:, head], wo_mid.at[head], local_sem.at[6])

    loop(8, lambda o: a_copy(o).start())
    a_local.start()

    for k in range(3):
        tell(token_sem.at[2 * k], up_dev)
        tell(token_sem.at[2 * k + 1], down_dev)
        pl.semaphore_wait(token_sem.at[2 * k], 1)
        pl.semaphore_wait(token_sem.at[2 * k + 1], 1)
    tell(token_sem.at[6], across_dev)
    pl.semaphore_wait(token_sem.at[6], 1)
    tell(token_sem.at[7], core_dev)
    pl.semaphore_wait(token_sem.at[7], 1)

    loads[4].wait()

    def add_squares(k, total):
        part = resid[:, pl.ds(pl.multiple_of(k * 512, 512), 512)].astype(jnp.float32)
        part = part * part
        return total + part[:, :128] + part[:, 128:256] + part[:, 256:384] + part[:, 384:]

    squares = lax.fori_loop(0, 16, add_squares, jnp.zeros((256, 128), jnp.float32))
    inv_ref[...] = lax.rsqrt(jnp.sum(squares, axis=1, keepdims=True) * (1.0 / 8192) + epsilon)

    loop(8, lambda o: a_arrival(o).wait_recv())
    a_local.wait()

    def b_copy(o):
        peer = rem(me + o, 32)
        return pltpu.make_async_remote_copy(
            src_ref=wo_mid.at[peer // 4, rem(peer, 4)], dst_ref=wo.at[head, me],
            send_sem=b_send.at[o], recv_sem=b_recv.at[me],
            device_id=(peer, head), device_id_type=MESH,
        )

    def b_arrival(o):
        peer = rem(me + o, 32)
        return pltpu.make_async_remote_copy(
            src_ref=wo_mid.at[peer // 4, rem(peer, 4)], dst_ref=wo.at[head, peer],
            send_sem=b_send.at[o], recv_sem=b_recv.at[peer],
            device_id=(peer, head), device_id_type=MESH,
        )

    b_local = pltpu.make_async_copy(
        wo_mid.at[me // 4, rem(me, 4)], wo.at[head, me], local_sem.at[7]
    )
    loop(32, lambda o: b_copy(o).start())
    b_local.start()

    acc[...] = jnp.zeros_like(acc)
    acc_kv[...] = jnp.zeros_like(acc_kv)
    acc_v[...] = jnp.zeros_like(acc_v)
    row = lax.broadcasted_iota(jnp.int32, (256, 256), 0)
    col = lax.broadcasted_iota(jnp.int32, (256, 256), 1)

    def column(values):
        return jnp.sum(jnp.where(row == col, values, 0.0), axis=1, keepdims=True)

    def project(chips, weights, total):
        for yy, zz in chips:
            at = pl.multiple_of((yy * 8 + zz) * 512, 512)
            part = resid[:, pl.ds(at, 512)].astype(jnp.float32)
            normed = (part * inv_ref[...] * gain_ref[:, pl.ds(at, 512)]).astype(jnp.bfloat16)
            total[...] += jnp.dot(
                normed, weights[yy, zz].reshape(512, -1), preferred_element_type=jnp.float32
            )

    def virtual_part(chips):
        for yy, zz in chips:
            for cc in range(2):
                j = seq_of(yy, zz, cc)
                gain = column(gain_ref[:, pl.ds(pl.multiple_of(j * 256, 256), 256)])
                scaled = (q_all[yy, zz, cc].astype(jnp.float32) * gain).astype(jnp.bfloat16)
                acc_v[...] += jnp.dot(
                    wo[:, j].reshape(128, 256), scaled, preferred_element_type=jnp.float32
                )

    def patch(chips):
        for yy, zz in chips:
            k = yy * 8 + zz
            rows = s_all[k // 2, :, pl.ds(pl.multiple_of(rem(k, 2) * 256, 256), 256)]
            acc[...] += inv_ref[...] * jnp.dot(
                rows, v_all[yy, zz].reshape(256, 512), preferred_element_type=jnp.float32
            )

    def take_q(chips):
        project(chips, q_all, acc)
        return chips

    def take_kv(chips):
        project(chips, kv_all, acc_kv)

    waiting = []
    qring.plane(1)
    loop(32, lambda o: b_arrival(o).wait_recv())
    b_local.wait()
    oring.start()
    waiting += take_q(qring.chips(0))
    oring.pair()
    qring.plane(2)
    waiting += take_q(qring.chips(1))
    oring.one(0)
    qring.other_start()
    qring.plane(3)
    oring.one(1)
    for k in (2, 3):
        loads[k].wait()
    kvring.start()
    loads[5].wait()
    sring.start()
    waiting += take_q(qring.chips(2))
    qring.other(1)
    qring.plane(4)
    waiting += take_q(qring.chips(3))
    qring.cross(0)
    qring.cross(1)
    qring.other(2)
    sring.pair()
    kvring.plane(1)
    waiting += take_q(qring.chips(4))
    oring.two(0)
    oring.two(1)
    virtual_part(waiting)
    qring.cross(2)
    qring.other(3)
    kvring.plane(2)
    for d in (0, 1, 2):
        virtual_part(take_q(qring.other_chips(d)))
    qring.cross(3)
    qring.other(4)
    qring.cross(4)
    kvring.other_start()
    sring.one(0)
    for d in (3, 4):
        virtual_part(take_q(qring.other_chips(d)))

    for r in range(4):
        cols = pl.ds(r * 128, 128)
        keep = edge_ref[me, head * 4 + r].astype(jnp.float32)
        v_all[y, z, c, :, cols] = (acc_v[:, cols] * keep).astype(jnp.bfloat16)
    vring.start()
    kvring.plane(3)
    sring.one(1)
    for d in (0, 1, 2):
        take_kv(kvring.chips(d))
    vring.plane(1)
    kvring.other(1)
    kvring.plane(4)
    vring.other_start()
    vring.plane(2)
    kvring.other(2)
    for d in (3, 4):
        take_kv(kvring.chips(d))
    sring.two(0)
    sring.two(1)
    patch(vring.chips(0))
    vring.other(1)
    vring.plane(3)
    kvring.other(3)
    patch(vring.chips(1))
    vring.other(2)
    vring.plane(4)
    for d in range(4):
        kvring.cross(d)
    kvring.other(4)
    kvring.cross(4)
    vring.cross(0)
    vring.cross(1)
    vring.other(3)
    patch(vring.chips(2))
    for d in range(5):
        take_kv(kvring.other_chips(d))
    patch(vring.other_chips(0))
    vring.cross(2)
    vring.other(4)
    patch(vring.chips(3))
    vring.cross(3)
    vring.cross(4)
    patch(vring.chips(4))
    keys = acc_kv[:, :128].astype(jnp.bfloat16)
    values = acc_kv[:, 128:].astype(jnp.bfloat16)
    for d in range(1, 5):
        patch(vring.other_chips(d))

    doc_row = doc_ref[...].astype(jnp.float32)
    allowed = (column(doc_row) == doc_row) & (col <= row)
    for r in range(4):
        cols = pl.ds(r * 128, 128)
        query = acc[:, cols].astype(jnp.bfloat16)
        scores = lax.dot_general(
            query, keys, (((1,), (1,)), ((), ())), preferred_element_type=jnp.float32
        ) * HEAD_SIZE ** (-0.5)
        scores = jnp.where(allowed, scores, -jnp.inf)
        weights = jnp.exp(scores - jnp.max(scores, axis=1, keepdims=True))
        weights = (weights / jnp.sum(weights, axis=1, keepdims=True)).astype(jnp.bfloat16)
        out_ref[:, cols] = jnp.dot(
            weights, values, preferred_element_type=jnp.float32
        ).astype(jnp.bfloat16)

    for ring in (qring, kvring, vring, oring, sring):
        ring.finish()
    loop(8, lambda o: a_copy(o).wait_send())
    loop(32, lambda o: b_copy(o).wait_send())


def local(resid, norm_gain, sender_diff, w_out1, w_query, w_key, w_value, edge_mask, doc_ids):
    dma = pltpu.SemaphoreType.DMA
    anywhere = pl.BlockSpec(memory_space=pl.ANY)
    vmem = pl.BlockSpec(memory_space=pltpu.VMEM)
    smem = pl.BlockSpec(memory_space=pltpu.SMEM)
    bf16, f32 = jnp.bfloat16, jnp.float32
    return pl.pallas_call(
        kernel,
        out_shape=jax.ShapeDtypeStruct((256, 512), bf16),
        in_specs=[
            anywhere, vmem, anywhere, anywhere, anywhere, anywhere, anywhere, smem, vmem,
        ],
        out_specs=vmem,
        scratch_shapes=[
            pltpu.VMEM((256, 8192), bf16),
            pltpu.VMEM((2, NZ, 2, 256, 512), bf16),
            pltpu.VMEM((2, NZ, 2, 256, 256), bf16),
            pltpu.VMEM((2, NZ, 2, 128, 512), bf16),
            pltpu.VMEM((8, 256, 512), bf16),
            pltpu.VMEM((8, 32, 16, 256), bf16),
            pltpu.VMEM((4, 8, 16, 256), bf16),
            pltpu.VMEM((8, 4, 16, 256), bf16),
            pltpu.VMEM((256, 512), f32),
            pltpu.VMEM((256, 256), f32),
            pltpu.VMEM((128, 512), f32),
            pltpu.VMEM((256, 1), f32),
            dma((8,)),
            pltpu.SemaphoreType.REGULAR((8,)),
            *[[dma((32,)), dma((32,)), dma((2,)), dma((52,))] for _ in range(3)],
            *[[dma((8,)), dma((2,)), dma((10,))] for _ in range(2)],
            dma((8,)), dma((8,)),
            dma((32,)), dma((32,)),
        ],
        compiler_params=pltpu.CompilerParams(
            collective_id=0, has_side_effects=True, vmem_limit_bytes=60 * 1024 * 1024
        ),
        name="patch_layer",
    )(
        resid,
        norm_gain.reshape(1, -1),
        sender_diff,
        w_out1.reshape(4, 8, 16, 256),
        w_query,
        w_key,
        w_value,
        edge_mask,
        doc_ids,
    )


def solution(mesh):
    placed = (
        P("seq", None),
        P(),
        P("seq", "head"),
        P("head", "seq"),
        P("seq", "head"),
        P("seq", "head"),
        P("seq", "head"),
        P(),
        P("seq", None),
    )
    return jax.shard_map(
        local, mesh=mesh, in_specs=placed, out_specs=P("seq", "head"), check_vma=False
    )
```

time: 126 us -> 106 us (0.84)
  the two profiles are of different devices: /device:TPU:25 before, /device:TPU:1 now
where the time goes in v2:
time: 106 us
  Pallas kernels  104 us (98%)
  local copies, waits for them, and re-layouts  1.67 us (2%)
    pallas_call x1, Pallas kernels, local(): pl.pallas_call(kernel, out_shape=jax.ShapeDtypeStruct((256, 512), bf16),...  104 us

profile of v2, /device:TPU:1, one launch (start us, length us, event | category | flops | bytes accessed | tf_op | source)
XLA Modules:
  0.0 106.1 jit_solution(14898979146701709393)
XLA Ops:
  0.0 104.4 %patch_layer.1 = bf16[256,512]{1,0:T(8,128)(2,1)} custom-call(bf16[256,8192]{1,0:T(8,128)(2,1)} %resid_hbm.1, f32[1,8192]{1,0:T(1,128)} %bitcast.3, bf16[256,512]{1,0:T(8,128)(2,1)} %sender_hbm.1, bf16[4,8,16,256]{3,2,1,0:T(8,128)(2,1)} %bitcast.2, bf16[256,512]{1,0:T(8,128)(2,1)} %wq_hbm.1, bf16[256,128]{1,0:T(8,128)(2,1)} %wk_hbm.1, ...), custom_call_target="tpu_custom_call" | custom-call | tf_op jit(solution)/shard_map/patch_layer/pallas_call | solution.py:468
  104.4 1.7 %copy.11 = bf16[256,512]{1,0:T(8,128)(2,1)} copy(bf16[256,512]{1,0:T(8,128)(2,1)} %patch_layer.1) | data formatting | bytes 524288

commit v3 on v2

--- a/solution.py
+++ b/solution.py
@@ -18,8 +18,8 @@
 def kernel(
     resid_hbm, gain_ref, sender_hbm, out1_hbm, wq_hbm, wk_hbm, wv_hbm, edge_ref, doc_ref,
     out_ref,
-    resid, q_all, kv_all, v_all, s_all, wo, wo_own, wo_mid, acc, acc_kv, acc_v, inv_ref,
-    local_sem, token_sem, q_sems, kv_sems, v_sems, wo_sems, s_sems,
+    resid, qa_all, qb_all, kv_all, v_all, s_all, wo, wo_own, wo_mid, acc, acc_kv, acc_v, inv_ref,
+    local_sem, token_sem, qa_sems, qb_sems, kv_sems, v_sems, wo_sems, s_sems,
     a_recv, a_send, b_recv, b_send,
 ):
     me = lax.axis_index("seq")
@@ -43,13 +43,14 @@
 
     loads = [
         pltpu.make_async_copy(out1_hbm, wo_own, local_sem.at[0]),
-        pltpu.make_async_copy(wq_hbm, q_all.at[y, z, c], local_sem.at[1]),
+        pltpu.make_async_copy(wq_hbm.at[:, pl.ds(0, 256)], qa_all.at[y, z, c], local_sem.at[1]),
         pltpu.make_async_copy(wk_hbm, kv_all.at[y, z, c, :, pl.ds(0, 128)], local_sem.at[2]),
         pltpu.make_async_copy(wv_hbm, kv_all.at[y, z, c, :, pl.ds(128, 128)], local_sem.at[3]),
         pltpu.make_async_copy(resid_hbm, resid, local_sem.at[4]),
         pltpu.make_async_copy(sender_hbm, s_all.at[head], local_sem.at[5]),
+        pltpu.make_async_copy(wq_hbm.at[:, pl.ds(256, 256)], qb_all.at[y, z, c], local_sem.at[8]),
     ]
-    for k in (1, 0, 2, 3, 4, 5):
+    for k in (1, 6, 0, 5, 4, 2, 3):
         loads[k].start()
 
     def loop(n, f):
@@ -70,8 +71,8 @@
     for device in (across_dev, up_dev, down_dev, core_dev):
         tell(barrier, device)
     loop(8, lambda o: tell(barrier, (me, rem(head + o, 8))))
-    loads[1].wait()
-    loads[0].wait()
+    for k in (1, 6, 0, 5):
+        loads[k].wait()
     pl.semaphore_wait(barrier, 11)
 
     class Ring:
@@ -230,12 +231,14 @@
             for copy in self.sent:
                 copy.wait_send()
 
-    qring = Ring(q_all, q_sems, 128)
+    qa_ring = Ring(qa_all, qa_sems, 128)
+    qb_ring = Ring(qb_all, qb_sems, 128)
     kvring = Ring(kv_all, kv_sems, 128)
     vring = Ring(v_all, v_sems, 64)
     oring = HeadRing(wo, wo_sems)
     sring = HeadRing(s_all, s_sems)
-    qring.start()
+    qa_ring.start()
+    qb_ring.start()
 
     def a_copy(o):
         peer = rem(head + o, 8)
@@ -257,6 +260,7 @@
 
     loop(8, lambda o: a_copy(o).start())
     a_local.start()
+    sring.start()
 
     for k in range(3):
         tell(token_sem.at[2 * k], up_dev)
@@ -312,24 +316,28 @@
     def column(values):
         return jnp.sum(jnp.where(row == col, values, 0.0), axis=1, keepdims=True)
 
-    def project(chips, weights, total):
+    def project(chips, pairs):
         for yy, zz in chips:
             at = pl.multiple_of((yy * 8 + zz) * 512, 512)
             part = resid[:, pl.ds(at, 512)].astype(jnp.float32)
             normed = (part * inv_ref[...] * gain_ref[:, pl.ds(at, 512)]).astype(jnp.bfloat16)
-            total[...] += jnp.dot(
-                normed, weights[yy, zz].reshape(512, -1), preferred_element_type=jnp.float32
-            )
+            for weights, total, cols in pairs:
+                total[:, cols] += jnp.dot(
+                    normed, weights[yy, zz].reshape(512, 256), preferred_element_type=jnp.float32
+                )
+
+    left, right = pl.ds(0, 256), pl.ds(256, 256)
 
     def virtual_part(chips):
         for yy, zz in chips:
             for cc in range(2):
                 j = seq_of(yy, zz, cc)
                 gain = column(gain_ref[:, pl.ds(pl.multiple_of(j * 256, 256), 256)])
-                scaled = (q_all[yy, zz, cc].astype(jnp.float32) * gain).astype(jnp.bfloat16)
-                acc_v[...] += jnp.dot(
-                    wo[:, j].reshape(128, 256), scaled, preferred_element_type=jnp.float32
-                )
+                for weights, cols in ((qa_all, left), (qb_all, right)):
+                    scaled = (weights[yy, zz, cc].astype(jnp.float32) * gain).astype(jnp.bfloat16)
+                    acc_v[:, cols] += jnp.dot(
+                        wo[:, j].reshape(128, 256), scaled, preferred_element_type=jnp.float32
+                    )
 
     def patch(chips):
         for yy, zz in chips:
@@ -339,12 +347,22 @@
                 rows, v_all[yy, zz].reshape(256, 512), preferred_element_type=jnp.float32
             )
 
+    class Both:
+        def __getattr__(self, name):
+            def call(*args):
+                getattr(qa_ring, name)(*args)
+                return getattr(qb_ring, name)(*args)
+
+            return call
+
+    qring = Both()
+
     def take_q(chips):
-        project(chips, q_all, acc)
+        project(chips, ((qa_all, acc, left), (qb_all, acc, right)))
         return chips
 
     def take_kv(chips):
-        project(chips, kv_all, acc_kv)
+        project(chips, ((kv_all, acc_kv, left),))
 
     waiting = []
     qring.plane(1)
@@ -352,41 +370,41 @@
     b_local.wait()
     oring.start()
     waiting += take_q(qring.chips(0))
-    oring.pair()
     qring.plane(2)
+    qring.other_start()
     waiting += take_q(qring.chips(1))
+    sring.pair()
     oring.one(0)
-    qring.other_start()
     qring.plane(3)
-    oring.one(1)
     for k in (2, 3):
         loads[k].wait()
     kvring.start()
-    loads[5].wait()
-    sring.start()
+    oring.pair()
+    qring.other(1)
+    sring.one(0)
     waiting += take_q(qring.chips(2))
-    qring.other(1)
     qring.plane(4)
+    kvring.plane(1)
+    qring.other(2)
     waiting += take_q(qring.chips(3))
+    oring.one(1)
+    sring.one(1)
+    kvring.plane(2)
     qring.cross(0)
     qring.cross(1)
-    qring.other(2)
-    sring.pair()
-    kvring.plane(1)
+    qring.other(3)
     waiting += take_q(qring.chips(4))
     oring.two(0)
+    kvring.other_start()
     oring.two(1)
     virtual_part(waiting)
+    kvring.plane(3)
     qring.cross(2)
-    qring.other(3)
-    kvring.plane(2)
+    qring.other(4)
     for d in (0, 1, 2):
         virtual_part(take_q(qring.other_chips(d)))
     qring.cross(3)
-    qring.other(4)
     qring.cross(4)
-    kvring.other_start()
-    sring.one(0)
     for d in (3, 4):
         virtual_part(take_q(qring.other_chips(d)))
 
@@ -395,31 +413,28 @@
         keep = edge_ref[me, head * 4 + r].astype(jnp.float32)
         v_all[y, z, c, :, cols] = (acc_v[:, cols] * keep).astype(jnp.bfloat16)
     vring.start()
-    kvring.plane(3)
-    sring.one(1)
+    kvring.other(1)
     for d in (0, 1, 2):
         take_kv(kvring.chips(d))
     vring.plane(1)
-    kvring.other(1)
     kvring.plane(4)
     vring.other_start()
+    kvring.other(2)
     vring.plane(2)
-    kvring.other(2)
     for d in (3, 4):
         take_kv(kvring.chips(d))
     sring.two(0)
     sring.two(1)
     patch(vring.chips(0))
+    kvring.other(3)
     vring.other(1)
     vring.plane(3)
-    kvring.other(3)
     patch(vring.chips(1))
+    kvring.other(4)
     vring.other(2)
     vring.plane(4)
-    for d in range(4):
+    for d in range(5):
         kvring.cross(d)
-    kvring.other(4)
-    kvring.cross(4)
     vring.cross(0)
     vring.cross(1)
     vring.other(3)
@@ -453,7 +468,7 @@
             weights, values, preferred_element_type=jnp.float32
         ).astype(jnp.bfloat16)
 
-    for ring in (qring, kvring, vring, oring, sring):
+    for ring in (qa_ring, qb_ring, kvring, vring, oring, sring):
         ring.finish()
     loop(8, lambda o: a_copy(o).wait_send())
     loop(32, lambda o: b_copy(o).wait_send())
@@ -474,7 +489,8 @@
         out_specs=vmem,
         scratch_shapes=[
             pltpu.VMEM((256, 8192), bf16),
-            pltpu.VMEM((2, NZ, 2, 256, 512), bf16),
+            pltpu.VMEM((2, NZ, 2, 256, 256), bf16),
+            pltpu.VMEM((2, NZ, 2, 256, 256), bf16),
             pltpu.VMEM((2, NZ, 2, 256, 256), bf16),
             pltpu.VMEM((2, NZ, 2, 128, 512), bf16),
             pltpu.VMEM((8, 256, 512), bf16),
@@ -485,9 +501,9 @@
             pltpu.VMEM((256, 256), f32),
             pltpu.VMEM((128, 512), f32),
             pltpu.VMEM((256, 1), f32),
-            dma((8,)),
+            dma((9,)),
             pltpu.SemaphoreType.REGULAR((8,)),
-            *[[dma((32,)), dma((32,)), dma((2,)), dma((52,))] for _ in range(3)],
+            *[[dma((32,)), dma((32,)), dma((2,)), dma((52,))] for _ in range(4)],
             *[[dma((8,)), dma((2,)), dma((10,))] for _ in range(2)],
             dma((8,)), dma((8,)),
             dma((32,)), dma((32,)),

time: 106 us -> 102 us (0.962)
  Pallas kernels: 104 us -> 99.7 us
    pallas_call x1, Pallas kernels: 104 us -> 99.7 us  [local(): pl.pallas_call(kernel, out_shape=jax.ShapeDtypeStruct((256, 512), bf16),...]
where the time goes in v3:
time: 102 us; the launch traced here: 101 us
  Pallas kernels  99.7 us (98%)
  local copies, waits for them, and re-layouts  1.67 us (2%)
    pallas_call x1, Pallas kernels, local(): pl.pallas_call(kernel, out_shape=jax.ShapeDtypeStruct((256, 512), bf16),...  99.7 us

profile of v3, /device:TPU:1, one launch (start us, length us, event | category | flops | bytes accessed | tf_op | source)
XLA Modules:
  0.0 101.4 jit_solution(9329452481230055390)
XLA Ops:
  0.0 99.7 %patch_layer.1 = bf16[256,512]{1,0:T(8,128)(2,1)} custom-call(bf16[256,8192]{1,0:T(8,128)(2,1)} %resid_hbm.1, f32[1,8192]{1,0:T(1,128)} %bitcast.3, bf16[256,512]{1,0:T(8,128)(2,1)} %sender_hbm.1, bf16[4,8,16,256]{3,2,1,0:T(8,128)(2,1)} %bitcast.2, bf16[256,512]{1,0:T(8,128)(2,1)} %wq_hbm.1, bf16[256,128]{1,0:T(8,128)(2,1)} %wk_hbm.1, ...), custom_call_target="tpu_custom_call" | custom-call | tf_op jit(solution)/shard_map/patch_layer/pallas_call | solution.py:483
  99.8 1.7 %copy.11 = bf16[256,512]{1,0:T(8,128)(2,1)} copy(bf16[256,512]{1,0:T(8,128)(2,1)} %patch_layer.1) | data formatting | bytes 524288

commit v4 on v3

--- a/solution.py
+++ b/solution.py
@@ -113,6 +113,9 @@
             self.put(slot, self.whole, down_dev, self.main(slot))
             self.put(slot, self.a, across_dev, self.main(slot))
             self.put(slot, self.whole, core_dev, self.main(slot))
+
+        def own_across(self):
+            slot = (y, z, c)
             self.put(slot, self.b, across_dev, self.late(slot))
 
         def round(self, yy, d, rows, kind):
@@ -237,9 +240,6 @@
     vring = Ring(v_all, v_sems, 64)
     oring = HeadRing(wo, wo_sems)
     sring = HeadRing(s_all, s_sems)
-    qa_ring.start()
-    qb_ring.start()
-
     def a_copy(o):
         peer = rem(head + o, 8)
         return pltpu.make_async_remote_copy(
@@ -260,6 +260,8 @@
 
     loop(8, lambda o: a_copy(o).start())
     a_local.start()
+    qa_ring.start()
+    qb_ring.start()
     sring.start()
 
     for k in range(3):
@@ -272,16 +274,6 @@
     tell(token_sem.at[7], core_dev)
     pl.semaphore_wait(token_sem.at[7], 1)
 
-    loads[4].wait()
-
-    def add_squares(k, total):
-        part = resid[:, pl.ds(pl.multiple_of(k * 512, 512), 512)].astype(jnp.float32)
-        part = part * part
-        return total + part[:, :128] + part[:, 128:256] + part[:, 256:384] + part[:, 384:]
-
-    squares = lax.fori_loop(0, 16, add_squares, jnp.zeros((256, 128), jnp.float32))
-    inv_ref[...] = lax.rsqrt(jnp.sum(squares, axis=1, keepdims=True) * (1.0 / 8192) + epsilon)
-
     loop(8, lambda o: a_arrival(o).wait_recv())
     a_local.wait()
 
@@ -306,6 +298,16 @@
     )
     loop(32, lambda o: b_copy(o).start())
     b_local.start()
+
+    loads[4].wait()
+
+    def add_squares(k, total):
+        part = resid[:, pl.ds(pl.multiple_of(k * 512, 512), 512)].astype(jnp.float32)
+        part = part * part
+        return total + part[:, :128] + part[:, 128:256] + part[:, 256:384] + part[:, 384:]
+
+    squares = lax.fori_loop(0, 16, add_squares, jnp.zeros((256, 128), jnp.float32))
+    inv_ref[...] = lax.rsqrt(jnp.sum(squares, axis=1, keepdims=True) * (1.0 / 8192) + epsilon)
 
     acc[...] = jnp.zeros_like(acc)
     acc_kv[...] = jnp.zeros_like(acc_kv)
@@ -369,6 +371,7 @@
     loop(32, lambda o: b_arrival(o).wait_recv())
     b_local.wait()
     oring.start()
+    qring.own_across()
     waiting += take_q(qring.chips(0))
     qring.plane(2)
     qring.other_start()
@@ -379,6 +382,7 @@
     for k in (2, 3):
         loads[k].wait()
     kvring.start()
+    kvring.own_across()
     oring.pair()
     qring.other(1)
     sring.one(0)
@@ -413,6 +417,7 @@
         keep = edge_ref[me, head * 4 + r].astype(jnp.float32)
         v_all[y, z, c, :, cols] = (acc_v[:, cols] * keep).astype(jnp.bfloat16)
     vring.start()
+    vring.own_across()
     kvring.other(1)
     for d in (0, 1, 2):
         take_kv(kvring.chips(d))

time: 102 us -> 99.7 us (0.977)
  Pallas kernels: 99.7 us -> 97.8 us
    pallas_call x1, Pallas kernels: 99.7 us -> 97.8 us  [local(): pl.pallas_call(kernel, out_shape=jax.ShapeDtypeStruct((256, 512), bf16),...]
where the time goes in v4:
time: 99.7 us; the launch traced here: 99.5 us
  Pallas kernels  97.8 us (98%)
  local copies, waits for them, and re-layouts  1.67 us (2%)
    pallas_call x1, Pallas kernels, local(): pl.pallas_call(kernel, out_shape=jax.ShapeDtypeStruct((256, 512), bf16),...  97.8 us

profile of v4, /device:TPU:1, one launch (start us, length us, event | category | flops | bytes accessed | tf_op | source)
XLA Modules:
  0.0 99.5 jit_solution(17534344642008567141)
XLA Ops:
  0.0 97.8 %patch_layer.1 = bf16[256,512]{1,0:T(8,128)(2,1)} custom-call(bf16[256,8192]{1,0:T(8,128)(2,1)} %resid_hbm.1, f32[1,8192]{1,0:T(1,128)} %bitcast.3, bf16[256,512]{1,0:T(8,128)(2,1)} %sender_hbm.1, bf16[4,8,16,256]{3,2,1,0:T(8,128)(2,1)} %bitcast.2, bf16[256,512]{1,0:T(8,128)(2,1)} %wq_hbm.1, bf16[256,128]{1,0:T(8,128)(2,1)} %wk_hbm.1, ...), custom_call_target="tpu_custom_call" | custom-call | tf_op jit(solution)/shard_map/patch_layer/pallas_call | solution.py:488
  97.8 1.7 %copy.11 = bf16[256,512]{1,0:T(8,128)(2,1)} copy(bf16[256,512]{1,0:T(8,128)(2,1)} %patch_layer.1) | data formatting | bytes 524288

commit v5 on v4

--- a/solution.py
+++ b/solution.py
@@ -234,9 +234,9 @@
             for copy in self.sent:
                 copy.wait_send()
 
-    qa_ring = Ring(qa_all, qa_sems, 128)
-    qb_ring = Ring(qb_all, qb_sems, 128)
-    kvring = Ring(kv_all, kv_sems, 128)
+    qa_ring = Ring(qa_all, qa_sems, 96)
+    qb_ring = Ring(qb_all, qb_sems, 96)
+    kvring = Ring(kv_all, kv_sems, 96)
     vring = Ring(v_all, v_sems, 64)
     oring = HeadRing(wo, wo_sems)
     sring = HeadRing(s_all, s_sems)

time: 99.7 us -> 104 us (1.043)
  Pallas kernels: 97.8 us -> 102 us
    pallas_call x1, Pallas kernels: 97.8 us -> 102 us  [local(): pl.pallas_call(kernel, out_shape=jax.ShapeDtypeStruct((256, 512), bf16),...]
where the time goes in v5:
time: 104 us
  Pallas kernels  102 us (98%)
  local copies, waits for them, and re-layouts  1.67 us (2%)
    pallas_call x1, Pallas kernels, local(): pl.pallas_call(kernel, out_shape=jax.ShapeDtypeStruct((256, 512), bf16),...  102 us

profile of v5, /device:TPU:1, one launch (start us, length us, event | category | flops | bytes accessed | tf_op | source)
XLA Modules:
  0.0 103.7 jit_solution(13741874344048001507)
XLA Ops:
  0.0 102.0 %patch_layer.1 = bf16[256,512]{1,0:T(8,128)(2,1)} custom-call(bf16[256,8192]{1,0:T(8,128)(2,1)} %resid_hbm.1, f32[1,8192]{1,0:T(1,128)} %bitcast.3, bf16[256,512]{1,0:T(8,128)(2,1)} %sender_hbm.1, bf16[4,8,16,256]{3,2,1,0:T(8,128)(2,1)} %bitcast.2, bf16[256,512]{1,0:T(8,128)(2,1)} %wq_hbm.1, bf16[256,128]{1,0:T(8,128)(2,1)} %wk_hbm.1, ...), custom_call_target="tpu_custom_call" | custom-call | tf_op jit(solution)/shard_map/patch_layer/pallas_call | solution.py:488
  102.0 1.7 %copy.11 = bf16[256,512]{1,0:T(8,128)(2,1)} copy(bf16[256,512]{1,0:T(8,128)(2,1)} %patch_layer.1) | data formatting | bytes 524288
